TPU v7x, 128 devices: a whole 4x4x4 slice. The times are simulated.
128 devices in a mesh: req: 32 (over z, x, core), mlp: 4 (over y).
Axes of the slice: x: 4, y: 4, z: 4, core: 2. Of those that a mesh axis runs over, the one named last changes fastest.
Arguments:
- residual_in: bfloat16 [32768, 1664], P('req'), may hold values from -6 to 6
- lengths: int32 [4096], P(('req', 'mlp')), may hold values from 0 to 16, as said below
- owners: int32 [4096], P(('req', 'mlp')), may hold values from 0 to 31, as said below
- merge_dest: int32 [32768], P('req'), may hold values from 0 to 255, as said below
- segment_ids: int32 [32768], P('req'), may hold values from 0 to 3, as said below
- norm2_gain: float32 [1664], replicated, may hold values from 0.5 to 1.5
- norm2_bias: float32 [1664], replicated, may hold values from -3 to 3
- up_weight: bfloat16 [4096, 1664], P('mlp'), may hold values from -0.15625 to 0.15625
- up_bias: float32 [4096], P('mlp'), may hold values from -3 to 3
- down_weight: bfloat16 [4096, 1664], P('mlp'), may hold values from -0.09375 to 0.09375
- down_bias: float32 [1664], replicated, may hold values from -3 to 3
- proj_weight: bfloat16 [6656, 1664], P('mlp'), may hold values from -0.078125 to 0.078125
- norm3_gain: float32 [1664], replicated, may hold values from 0.5 to 1.5
- norm3_bias: float32 [1664], replicated, may hold values from -3 to 3
- next_weight: bfloat16 [1664, 3, 1664], P('req'), may hold values from -0.15625 to 0.15625
Outputs:
- merged_out: bfloat16 [16384, 1664], P(('req', 'mlp'))
- next_mixed: bfloat16 [16384, 1664], P(('req', 'mlp'))
Inputs may be any that keep to these rules, and one draw needn't show every extreme that they name: The 32 pieces of each block of 256 tokens (one device, req-major order) have lengths that are multiples of 4 and sum to 256; in every block one piece has exactly 16 tokens. The owners of the 32 pieces of one block are a permutation of 0 to 31; for each index of mlp, one piece of 16 tokens of each block of that index goes to one owner shared by all blocks of that index. `merge_dest`: within each device block a permutation of 0 to 255 that maps the tokens of each piece onto that piece's own positions. `segment_ids`: the four tokens of a block whose merge_dest values have the same quotient by 4 carry one segment id.
All inputs are finite; a program needn't handle non-finite values.
Results may differ from a plain program's by a relative error of at most 0.023.
Values may be sent and summed in bfloat16 or wider, within the bound.
No kernel may reach another device: no remote copies, remote signals or barrier semaphores. Data moves between devices by JAX's collectives and lax.ppermute only.
A program may use at most 128 MiB of HBM per device.

v0:
```python
import math
import jax
import jax.numpy as jnp
from jax import lax
from jax.sharding import PartitionSpec as P

HEAD_DIM = 104
EPSILON = 1e-06


def layer_norm(rows, gain, bias):
    values = rows.astype(jnp.float32)
    mean_value = jnp.mean(values, axis=-1, keepdims=True)
    centred = values - mean_value
    spread = jnp.mean(centred * centred, axis=-1, keepdims=True)
    return centred * lax.rsqrt(spread + EPSILON) * gain + bias


def block_attention(heads_in, slot_tags):
    queries = heads_in[:, :, 0]
    key_rows = heads_in[:, :, 1]
    value_rows = heads_in[:, :, 2]
    score_scale = 1.0 / math.sqrt(heads_in.shape[-1])
    scores = (
        jnp.einsum("bqhe,bkhe->bhqk", queries, key_rows, preferred_element_type=jnp.float32)
        * score_scale
    )
    slot_total = heads_in.shape[1]
    itself = lax.broadcasted_iota(jnp.int32, (slot_total, slot_total), 0) == lax.broadcasted_iota(
        jnp.int32, (slot_total, slot_total), 1
    )
    live_slots = slot_tags >= 0
    same_request = slot_tags[:, :, None] == slot_tags[:, None, :]
    allowed = same_request & live_slots[:, None, :] | itself[None]
    weights = jnp.where(allowed[:, None], jnp.exp(scores), 0.0)
    probs = (weights / jnp.sum(weights, axis=-1, keepdims=True)).astype(jnp.bfloat16)
    mixed_out = jnp.einsum("bhqk,bkhe->bqhe", probs, value_rows, preferred_element_type=jnp.float32)
    mixed_out = jnp.where(live_slots[:, :, None, None], mixed_out, 0.0)
    return mixed_out.astype(jnp.bfloat16)


def body(
    residual_in,
    lengths,
    owners,
    merge_dest,
    segment_ids,
    norm2_gain,
    norm2_bias,
    up_weight,
    up_bias,
    down_weight,
    down_bias,
    proj_weight,
    norm3_gain,
    norm3_bias,
    next_weight,
):
    group_rows, model_width = residual_in.shape
    lane_count = lax.axis_size("mlp")
    sender_count = lax.axis_size("req")
    lane_index = lax.axis_index("mlp")
    own_rows = group_rows // lane_count
    merged_rows = own_rows // 4
    slot_count = 2 * merged_rows // sender_count
    normed = layer_norm(residual_in, norm2_gain, norm2_bias).astype(jnp.bfloat16)
    upward = lax.dot_general(
        normed, up_weight, (((1,), (1,)), ((), ())), preferred_element_type=jnp.float32
    )
    hidden = jax.nn.gelu(upward + up_bias, approximate=False).astype(jnp.bfloat16)
    partial_sums = jnp.dot(hidden, down_weight, preferred_element_type=jnp.float32)
    places = merge_dest.reshape(lane_count, own_rows)
    block_ids = lax.broadcasted_iota(jnp.int32, (lane_count, own_rows), 0)
    token_ids = lax.broadcasted_iota(jnp.int32, (lane_count, own_rows), 1)
    sources = jnp.zeros((lane_count, own_rows), jnp.int32).at[block_ids, places].set(token_ids)
    block_offset = own_rows * lax.broadcasted_iota(jnp.int32, (lane_count, merged_rows, 4), 0)
    group_index = sources.reshape(lane_count, merged_rows, 4) + block_offset
    quadrant_rows = lax.dynamic_index_in_dim(group_index, lane_index, 2, False).reshape(-1)
    feed_out = lax.psum(partial_sums.astype(jnp.bfloat16), "mlp").astype(jnp.float32)
    layer_out = (residual_in.astype(jnp.float32) + feed_out + down_bias).astype(jnp.bfloat16)
    quarter = jnp.take(layer_out, quadrant_rows, axis=0)
    projected = lax.psum_scatter(
        jnp.dot(quarter, proj_weight, preferred_element_type=jnp.float32).astype(jnp.bfloat16),
        "mlp",
        scatter_dimension=0,
        tiled=True,
    )
    first_tokens = lax.dynamic_index_in_dim(group_index[:, :, 0], lane_index, 0, False)
    row_segment = jnp.take(segment_ids, first_tokens, axis=0)
    counts = lengths // 4
    starts = jnp.cumsum(counts) - counts
    index = lax.broadcasted_iota(jnp.int32, (merged_rows, 1), 0)
    inside = ((index >= starts[None, :]) & (index < (starts + counts)[None, :])).astype(jnp.int32)
    owner_of = jnp.sum(inside * owners[None, :], axis=1)
    rank = index[:, 0] - jnp.sum(inside * starts[None, :], axis=1)
    target = owner_of * slot_count + rank
    slot_ids = lax.broadcasted_iota(jnp.int32, (sender_count * slot_count, 1), 0)
    route_hits = slot_ids == target[None, :]
    outgoing = jnp.dot(
        route_hits.astype(jnp.bfloat16), projected, preferred_element_type=jnp.float32
    ).astype(jnp.bfloat16)
    sent_tags = jnp.sum(route_hits.astype(jnp.int32) * (row_segment + 1)[None, :], axis=1) - 1
    received, arrived_tags = (
        lax.all_to_all(outgoing, "req", split_axis=0, concat_axis=0, tiled=True),
        lax.all_to_all(sent_tags, "req", split_axis=0, concat_axis=0, tiled=True),
    )
    normed3 = layer_norm(received, norm3_gain, norm3_bias).astype(jnp.bfloat16)
    recv_rows = received.shape[0]
    piece = lax.all_gather(next_weight, "req", axis=0, tiled=True)
    heads_in = jnp.dot(
        normed3, piece.reshape(piece.shape[0], -1), preferred_element_type=jnp.float32
    )
    heads_in = heads_in.astype(jnp.bfloat16).reshape(1, recv_rows, 3, -1, HEAD_DIM)
    next_mixed = block_attention(heads_in, arrived_tags.reshape(1, recv_rows)).reshape(
        recv_rows, model_width
    )
    return (received, next_mixed)


def solution(mesh):
    return jax.shard_map(
        body,
        mesh=mesh,
        in_specs=(
            P("req", None),
            P(("req", "mlp")),
            P(("req", "mlp")),
            P("req"),
            P("req"),
            P(),
            P(),
            P("mlp", None),
            P("mlp"),
            P("mlp", None),
            P(),
            P("mlp", None),
            P(),
            P(),
            P("req", None, None),
        ),
        out_specs=(P(("req", "mlp"), None), P(("req", "mlp"), None)),
        check_vma=False,
    )
```

profile of v0, /device:TPU:1, one launch (start us, length us, event | category | flops | bytes accessed | tf_op | source)
XLA Modules:
  0.0 286.2 jit_solution(13230346240546526583)
XLA Ops:
  8.1 2.6 convert_reduce_fusion
  11.2 1.0 fusion.2
  12.3 20.5 %convolution_convert_fusion.1 = bf16[1024,1664]{1,0:T(8,128)(2,1)} fusion(bf16[1024,1664]{1,0:T(8,128)(2,1)S(1)} %copy-done, bf16[1024,1664]{1,0:T(8,128)(2,1)} %param.22, bf16[1024,1664]{1,0:T(8,128)(2,1)} %param.15, f32[1664]{0:T(1024)S(1)} %copy-done.13, f32[1664]{0:T(1024)S(1)} %copy-done.14, f32[1024]{0:T(1024)S(1)} %add_rsqrt_fusion.1, ...), kind=kOutput, calls=%fused_computation.34 | convolution fusion | flops 7060455424 | bytes 13657088 | tf_op jit(solution)/shard_map/dot_general | solution.py:71
  33.2 4.5 %scatter_custom_fusion = s32[1024]{0:T(1024)S(1)} fusion(s32[1024]{0:T(1024)S(1)} %bitcast.53, s32[1024]{0:T(1024)S(1)} %bitcast.54, s32[]{:T(128)} %constant.46.clone.1), kind=kCustom, calls=%fused_computation.124 | custom fusion | bytes 4100
  39.6 76.7 %all-reduce.2.cloned.1.call-done = bf16[1024,1664]{1,0:T(8,128)(2,1)} async-done(((bf16[1024,1664]{1,0:T(8,128)(2,1)}), bf16[1024,1664]{1,0:T(8,128)(2,1)}) %all-reduce.2.cloned.1.call-update) | async-done | bytes 3407888 | tf_op jit(solution)/shard_map/psum | solution.py:79
  116.3 4.8 %fusion.7 = bf16[1024,1664]{1,0:T(8,128)(2,1)} fusion(bf16[1024,1664]{1,0:T(8,128)(2,1)S(1)} %copy-done.4, bf16[1024,1664]{1,0:T(8,128)(2,1)} %all-reduce.2.cloned.1.call-done, f32[1664]{0:T(1024)S(1)} %copy-done.8), kind=kLoop, calls=%fused_computation.13 | loop fusion | flops 8519680 | bytes 10230272 | tf_op jit(solution)/shard_map/convert_element_type | solution.py:80
  121.1 4.5 %gather_fusion = bf16[256,1664]{1,0:T(8,128)(2,1)S(1)} fusion(bf16[1024,1664]{1,0:T(8,128)(2,1)} %fusion.7, s32[1024]{0:T(1024)S(1)} %pad_clamp_fusion.1), kind=kCustom, calls=%fused_computation | custom fusion | bytes 1704960 | tf_op jit(solution)/shard_map/jit(_take)/gather | solution.py:81
  125.7 5.5 %convolution_convert_fusion.2 = bf16[256,1664]{1,0:T(8,128)(2,1)} fusion(bf16[1664,1664]{1,0:T(8,128)(2,1)} %param.26, bf16[256,1664]{1,0:T(8,128)(2,1)S(1)} %gather_fusion, pred[256]{0:T(512)(128)(4,1)S(1)} %compare_and_fusion), kind=kOutput, calls=%fused_computation.40 | convolution fusion | flops 1418526720 | bytes 7241984 | tf_op jit(solution)/shard_map/dot_general | solution.py:83
  131.2 1.1 copy.42
  132.8 0.7 gather_fusion.1
  133.9 14.4 %all_to_all.21 = s32[32,4,1]{1,2,0:T(1,128)S(1)} all-to-all(s32[32,4,1]{1,2,0:T(1,128)S(1)} %bitcast.51), channel_id=1, replica_groups=mesh['req'=32,'mlp'=4] {'req'}, dimensions={0} | all-to-all | bytes 1024 | tf_op jit(solution)/shard_map/all_to_all | solution.py:105
  149.6 3.1 %reduce-scatter.2.cloned.1.call-done = bf16[64,1664]{1,0:T(8,128)(2,1)} async-done(((bf16[256,1664]{1,0:T(8,128)(2,1)}), bf16[64,1664]{1,0:T(8,128)(2,1)}) %reduce-scatter.2.cloned.1.call-update) | async-done | bytes 213008 | tf_op jit(solution)/shard_map/reduce_scatter | solution.py:82
  152.7 1.3 convolution_convert_fusion.3
  154.0 0.9 all_to_all.14
  154.9 8.8 %all-to-all-start = ((bf16[32,4,1664]{2,1,0:T(4,128)(2,1)}), bf16[32,4,1664]{2,1,0:T(4,128)(2,1)S(1)}, u32[]{:S(2)}, u32[]{:S(2)}) async-start(bf16[32,4,1664]{2,1,0:T(4,128)(2,1)} %all_to_all.14), calls=%async_computation.1 | async-start | bytes 851968 | tf_op jit(solution)/shard_map/all_to_all | solution.py:104
  163.9 10.4 %all-to-all-done = bf16[32,4,1664]{2,1,0:T(4,128)(2,1)S(1)} async-done(((bf16[32,4,1664]{2,1,0:T(4,128)(2,1)}), bf16[32,4,1664]{2,1,0:T(4,128)(2,1)S(1)}, u32[]{:S(2)}, u32[]{:S(2)}) %all-to-all-start) | async-done | bytes 426016 | tf_op jit(solution)/shard_map/all_to_all | solution.py:104
  175.5 0.9 all_to_all.16
  176.4 44.4 %all-gather.2.cloned.1.call-done = bf16[1664,3,1664]{2,1,0:T(4,128)(2,1)} async-done(((bf16[52,3,1664]{2,1,0:T(4,128)(2,1)}), bf16[1664,3,1664]{2,1,0:T(4,128)(2,1)}) %all-gather.2.cloned.1.call-update) | async-done | bytes 16613392 | tf_op jit(solution)/shard_map/all_gather | solution.py:109
  220.8 36.4 %copy.43 = bf16[1664,3,1664]{0,2,1:T(8,128)(2,1)} copy(bf16[1664,3,1664]{2,1,0:T(4,128)(2,1)} %all-gather.2.cloned.1.call-done) | data formatting | bytes 33226752 | tf_op jit(solution)/shard_map/all_gather | solution.py:109
  257.2 11.7 %convolution_convert_fusion = bf16[128,4992]{1,0:T(8,128)(2,1)} fusion(bf16[128,1664]{1,0:T(8,128)(2,1)S(1)} %convert_element_type.63, bf16[1664,4992]{0,1:T(8,128)(2,1)} %bitcast.47), kind=kOutput, calls=%fused_computation.15 | convolution fusion | flops 2127151104 | bytes 18317312 | tf_op jit(solution)/shard_map/dot_general | solution.py:110
  268.8 2.6 copy.44
  271.4 2.5 fusion.60
  273.9 2.8 fusion.62
  276.8 2.0 copy.46
  (85 shorter events, 6.1 us)
Async XLA Ops:
  8.0 4.3 %copy-start = (bf16[1024,1664]{1,0:T(8,128)(2,1)S(1)}, bf16[1024,1664]{1,0:T(8,128)(2,1)}, u32[]{:S(2)}) copy-start(bf16[1024,1664]{1,0:T(8,128)(2,1)} %param.24) | copy-start | bytes 10223620
  8.0 4.3 %copy-start.15 = (f32[1024]{0:T(1024)S(1)}, f32[1024]{0:T(1024)}, u32[]{:S(2)}) copy-start(f32[1024]{0:T(1024)} %param.23) | copy-start | bytes 12292
  8.0 4.3 %copy-start.13 = (f32[1664]{0:T(1024)S(1)}, f32[1664]{0:T(1024)}, u32[]{:S(2)}) copy-start(f32[1664]{0:T(1024)} %param.21) | copy-start | bytes 19972
  8.0 108.3 %all-reduce.2.cloned.1.call-start = ((), (), s32[]{:S(2)}) async-start(), calls=%async_computation.3 | async-start | bytes 6815744 | tf_op jit(solution)/shard_map/psum | solution.py:79
  8.1 3.1 %copy-start.3 = (bf16[1024,1664]{1,0:T(8,128)(2,1)S(1)}, bf16[1024,1664]{1,0:T(8,128)(2,1)}, u32[]{:S(2)}) copy-start(bf16[1024,1664]{1,0:T(8,128)(2,1)} %param.15) | copy-start | bytes 10223620
  8.1 4.2 %copy-start.14 = (f32[1664]{0:T(1024)S(1)}, f32[1664]{0:T(1024)}, u32[]{:S(2)}) copy-start(f32[1664]{0:T(1024)} %param.20) | copy-start | bytes 19972
  12.3 20.6 %copy-start.9 = (s32[1024]{0:T(1024)S(1)}, s32[1024]{0:T(1024)}, u32[]{:S(2)}) copy-start(s32[1024]{0:T(1024)} %param.18) | copy-start | bytes 12292
  12.3 20.7 %copy-start.12 = (s32[2]{0:T(128)S(1)}, s32[2]{0:T(128)}, u32[]{:S(2)}) copy-start(s32[2]{0:T(128)} %constant.153) | copy-start | bytes 28
  12.3 20.7 %copy-start.11 = (s32[2]{0:T(128)S(1)}, s32[2]{0:T(128)}, u32[]{:S(2)}) copy-start(s32[2]{0:T(128)} %constant.156) | copy-start | bytes 28
  32.9 83.4 %copy-start.4 = (bf16[1024,1664]{1,0:T(8,128)(2,1)S(1)}, bf16[1024,1664]{1,0:T(8,128)(2,1)}, u32[]{:S(2)}) copy-start(bf16[1024,1664]{1,0:T(8,128)(2,1)} %param.15) | copy-start | bytes 10223620
  32.9 83.4 %copy-start.8 = (f32[1664]{0:T(1024)S(1)}, f32[1664]{0:T(1024)}, u32[]{:S(2)}) copy-start(f32[1664]{0:T(1024)} %param.25) | copy-start | bytes 19972
  32.9 119.8 %reduce-scatter.2.cloned.1.call-start = ((), (), s32[]{:S(2)}) async-start(), calls=%async_computation.4 | async-start | bytes 1064960 | tf_op jit(solution)/shard_map/reduce_scatter | solution.py:82
  125.6 5.6 %copy-start.5 = (bf16[52,3,1664]{2,0,1:T(8,128)(2,1)S(1)}, bf16[52,3,1664]{2,0,1:T(8,128)(2,1)}, u32[]{:S(2)}) copy-start(bf16[52,3,1664]{2,0,1:T(8,128)(2,1)} %param.29) | copy-start | bytes 1557508
  125.6 6.8 %copy-start.16 = (s32[32]{0:T(128)S(1)}, s32[32]{0:T(128)}, u32[]{:S(2)}) copy-start(s32[32]{0:T(128)} %param.16) | copy-start | bytes 388
  125.7 7.2 %copy-start.2 = (s32[1024]{0:T(1024)S(1)}, s32[1024]{0:T(1024)}, u32[]{:S(2)}) copy-start(s32[1024]{0:T(1024)} %param.19) | copy-start | bytes 12292
  125.7 7.9 %copy-start.10 = (s32[32]{0:T(128)S(1)}, s32[32]{0:T(128)}, u32[]{:S(2)}) copy-start(s32[32]{0:T(128)} %param.17) | copy-start | bytes 388
  131.2 43.8 %copy-start.6 = (f32[1664]{0:T(1024)S(1)}, f32[1664]{0:T(1024)}, u32[]{:S(2)}) copy-start(f32[1664]{0:T(1024)} %param.28) | copy-start | bytes 19972
  131.2 43.8 %copy-start.7 = (f32[1664]{0:T(1024)S(1)}, f32[1664]{0:T(1024)}, u32[]{:S(2)}) copy-start(f32[1664]{0:T(1024)} %param.27) | copy-start | bytes 19972
  131.2 89.6 %all-gather.2.cloned.1.call-start = ((), (), s32[]{:S(2)}) async-start(), calls=%async_computation.5 | async-start | bytes 22843392 | tf_op jit(solution)/shard_map/all_gather | solution.py:109
  154.9 19.4 %all-to-all-start = ((bf16[32,4,1664]{2,1,0:T(4,128)(2,1)}), bf16[32,4,1664]{2,1,0:T(4,128)(2,1)S(1)}, u32[]{:S(2)}, u32[]{:S(2)}) async-start(bf16[32,4,1664]{2,1,0:T(4,128)(2,1)} %all_to_all.14), calls=%async_computation.1 | async-start | bytes 851968 | tf_op jit(solution)/shard_map/all_to_all | solution.py:104
  268.8 9.9 %copy-start.1 = (bf16[1024,1664]{1,0:T(8,128)(2,1)S(1)}, bf16[1024,1664]{1,0:T(8,128)(2,1)}, u32[]{:S(2)}) copy-start(bf16[1024,1664]{1,0:T(8,128)(2,1)} %param.24) | copy-start | bytes 10223620
Sparse Core Ops, SparseCore 0:
  33.0 83.2 all-reduce.1
  131.3 21.3 reduce-scatter.1
Sparse Core Ops, SparseCore 1:
  134.3 86.4 all-gather.1
where the time goes:
time: 288 us; the launch traced here: 286 us
  waiting for transfers between devices  135 us (47%)
  local copies, waits for them, and re-layouts  56.2 us (20%)
  matrix products  44.3 us (15%)
  between operations  15.9 us (6%)
  blocking collectives  14.4 us (5%)
  other arithmetic  11.7 us (4%)
  starting transfers between devices  8.95 us (3%)
    psum x1, waiting for transfers between devices, body(): lax.psum(partial_sums.astype(jnp.bfloat16), 'mlp').astype(jnp.float32)  76.7 us
    all_gather x1, waiting for transfers between devices, body(): piece = lax.all_gather(next_weight, 'req', axis=0, tiled=True)  44.4 us
    all_gather x1, local copies, waits for them, and re-layouts, body(): piece = lax.all_gather(next_weight, 'req', axis=0, tiled=True)  36.4 us
    dot_general x1, matrix products, body(): jnp.dot(hidden, down_weight, preferred_element_type=jnp.float32)  20.5 us
    all_to_all x1, blocking collectives, body(): lax.all_to_all(sent_tags, 'req', split_axis=0, concat_axis=0, tiled=True)  14.4 us
    dot_general x1, matrix products, body(): jnp.dot(normed3, piece.reshape(piece.shape[0], -1), preferred_element_typ...  11.7 us
    all_to_all x1, waiting for transfers between devices, body(): lax.all_to_all(outgoing, 'req', split_axis=0, concat_axis=0, tiled=True)  10.4 us
    all_to_all x1, starting transfers between devices, body(): lax.all_to_all(outgoing, 'req', split_axis=0, concat_axis=0, tiled=True)  8.83 us
  transfers between devices with their start and end apart: 4, of which 4 were waited for; matrix products, arithmetic and copies ran while one was open for 5% of the time, Pallas kernels for 0%

commit v1 on v0

--- a/solution.py
+++ b/solution.py
@@ -76,7 +76,9 @@
     block_offset = own_rows * lax.broadcasted_iota(jnp.int32, (lane_count, merged_rows, 4), 0)
     group_index = sources.reshape(lane_count, merged_rows, 4) + block_offset
     quadrant_rows = lax.dynamic_index_in_dim(group_index, lane_index, 2, False).reshape(-1)
-    feed_out = lax.psum(partial_sums.astype(jnp.bfloat16), "mlp").astype(jnp.float32)
+    feed_out = jnp.sum(lax.all_gather(partial_sums.astype(jnp.bfloat16), "mlp"), axis=0).astype(
+        jnp.float32
+    )
     layer_out = (residual_in.astype(jnp.float32) + feed_out + down_bias).astype(jnp.bfloat16)
     quarter = jnp.take(layer_out, quadrant_rows, axis=0)
     projected = lax.psum_scatter(

time: 288 us -> 346 us (1.20)
  waiting for transfers between devices: 135 us -> 184 us
  other arithmetic: 11.7 us -> 20.7 us
    all_gather x0 -> x1, waiting for transfers between devices: none -> 125 us  [body(): lax.all_gather(partial_sums.astype(jnp.bfloat16), 'mlp')]
    psum x1 -> x0, waiting for transfers between devices: 76.7 us -> none  [body(): lax.psum(partial_sums.astype(jnp.bfloat16), 'mlp').astype(jnp.float32)]
    reduce_sum x0 -> x1, other arithmetic: none -> 9.72 us  [body(): jnp.sum(lax.all_gather(partial_sums.astype(jnp.bfloat16), 'mlp'), axis=0)]
  transfers between devices with their start and end apart: 4 -> 4, of which waited for: 4 -> 4; matrix products, arithmetic and copies ran while one was open for 5% -> 3% of each run, Pallas kernels for 0% -> 0%
where the time goes in v1:
time: 346 us; the launch traced here: 344 us
  waiting for transfers between devices  184 us (53%)
  local copies, waits for them, and re-layouts  55.7 us (16%)
  matrix products  44.3 us (13%)
  other arithmetic  20.7 us (6%)
  between operations  15.9 us (5%)
  blocking collectives  14.4 us (4%)
  starting transfers between devices  8.96 us (3%)
    all_gather x1, waiting for transfers between devices, body(): lax.all_gather(partial_sums.astype(jnp.bfloat16), 'mlp')  125 us
    all_gather x1, waiting for transfers between devices, body(): piece = lax.all_gather(next_weight, 'req', axis=0, tiled=True)  44.4 us
    all_gather x1, local copies, waits for them, and re-layouts, body(): piece = lax.all_gather(next_weight, 'req', axis=0, tiled=True)  36.4 us
    dot_general x1, matrix products, body(): jnp.dot(hidden, down_weight, preferred_element_type=jnp.float32)  20.4 us
    all_to_all x1, blocking collectives, body(): lax.all_to_all(sent_tags, 'req', split_axis=0, concat_axis=0, tiled=True)  14.4 us
    dot_general x1, matrix products, body(): jnp.dot(normed3, piece.reshape(piece.shape[0], -1), preferred_element_typ...  11.7 us
    all_to_all x1, waiting for transfers between devices, body(): lax.all_to_all(outgoing, 'req', split_axis=0, concat_axis=0, tiled=True)  10.4 us
    reduce_sum x1, other arithmetic, body(): jnp.sum(lax.all_gather(partial_sums.astype(jnp.bfloat16), 'mlp'), axis=0)  9.72 us
  transfers between devices with their start and end apart: 4, of which 4 were waited for; matrix products, arithmetic and copies ran while one was open for 3% of the time, Pallas kernels for 0%

profile of v1, /device:TPU:1, one launch (start us, length us, event | category | flops | bytes accessed | tf_op | source)
XLA Modules:
  0.0 344.3 jit_solution(9405995481612286250)
XLA Ops:
  8.1 2.6 convert_reduce_fusion
  11.2 1.0 fusion.2
  12.3 20.4 %convolution_convert_fusion.1 = bf16[1024,1664]{1,0:T(8,128)(2,1)} fusion(bf16[1024,1664]{1,0:T(8,128)(2,1)S(1)} %copy-done, bf16[1024,1664]{1,0:T(8,128)(2,1)} %param.22, bf16[1024,1664]{1,0:T(8,128)(2,1)} %param.15, f32[1664]{0:T(1024)S(1)} %copy-done.13, f32[1664]{0:T(1024)S(1)} %copy-done.14, f32[1024]{0:T(1024)S(1)} %add_rsqrt_fusion.1, ...), kind=kOutput, calls=%fused_computation.34 | convolution fusion | flops 7060455424 | bytes 13657088 | tf_op jit(solution)/shard_map/dot_general | solution.py:71
  33.1 4.5 %scatter_custom_fusion = s32[1024]{0:T(1024)S(1)} fusion(s32[1024]{0:T(1024)S(1)} %bitcast.55, s32[1024]{0:T(1024)S(1)} %bitcast.56, s32[]{:T(128)} %constant.47.clone.1), kind=kCustom, calls=%fused_computation.124 | custom fusion | bytes 4100
  38.3 125.4 %all-gather.6.cloned.1.call-done = bf16[4096,1664]{1,0:T(8,128)(2,1)} async-done(((bf16[1024,1664]{1,0:T(8,128)(2,1)}), bf16[4096,1664]{1,0:T(8,128)(2,1)}) %all-gather.6.cloned.1.call-update) | async-done | bytes 13631504 | tf_op jit(solution)/shard_map/all_gather | solution.py:79
  163.6 9.7 %reduce_sum.88 = bf16[1024,1664]{1,0:T(8,128)(2,1)} reduce(bf16[4,1024,1664]{2,1,0:T(8,128)(2,1)} %bitcast.49, bf16[]{:T(256)} %constant.148.clone.1), dimensions={0}, to_apply=%region_6.7 | reduce | flops 5111808 | bytes 17039362 | tf_op jit(solution)/shard_map/reduce_sum | solution.py:79
  173.4 4.7 %fusion.7 = bf16[1024,1664]{1,0:T(8,128)(2,1)} fusion(bf16[1024,1664]{1,0:T(8,128)(2,1)S(1)} %copy-done.4, bf16[1024,1664]{1,0:T(8,128)(2,1)} %reduce_sum.88, f32[1664]{0:T(1024)S(1)} %copy-done.8), kind=kLoop, calls=%fused_computation.13 | loop fusion | flops 8519680 | bytes 10230272 | tf_op jit(solution)/shard_map/convert_element_type | solution.py:82
  178.1 4.5 %gather_fusion = bf16[256,1664]{1,0:T(8,128)(2,1)S(1)} fusion(bf16[1024,1664]{1,0:T(8,128)(2,1)} %fusion.7, s32[1024]{0:T(1024)S(1)} %pad_clamp_fusion.1), kind=kCustom, calls=%fused_computation | custom fusion | bytes 1704960 | tf_op jit(solution)/shard_map/jit(_take)/gather | solution.py:83
  182.7 5.5 %convolution_convert_fusion.2 = bf16[256,1664]{1,0:T(8,128)(2,1)} fusion(bf16[1664,1664]{1,0:T(8,128)(2,1)} %param.26, bf16[256,1664]{1,0:T(8,128)(2,1)S(1)} %gather_fusion, pred[256]{0:T(512)(128)(4,1)S(1)} %compare_and_fusion), kind=kOutput, calls=%fused_computation.40 | convolution fusion | flops 1418526720 | bytes 7241984 | tf_op jit(solution)/shard_map/dot_general | solution.py:85
  188.2 1.1 copy.42
  190.9 14.4 %all_to_all.21 = s32[32,4,1]{1,2,0:T(1,128)S(1)} all-to-all(s32[32,4,1]{1,2,0:T(1,128)S(1)} %bitcast.53), channel_id=1, replica_groups=mesh['req'=32,'mlp'=4] {'req'}, dimensions={0} | all-to-all | bytes 1024 | tf_op jit(solution)/shard_map/all_to_all | solution.py:107
  206.6 4.2 %reduce-scatter.2.cloned.1.call-done = bf16[64,1664]{1,0:T(8,128)(2,1)} async-done(((bf16[256,1664]{1,0:T(8,128)(2,1)}), bf16[64,1664]{1,0:T(8,128)(2,1)}) %reduce-scatter.2.cloned.1.call-update) | async-done | bytes 213008 | tf_op jit(solution)/shard_map/reduce_scatter | solution.py:84
  210.9 1.3 convolution_convert_fusion.3
  212.2 0.9 all_to_all.14
  213.1 8.8 %all-to-all-start = ((bf16[32,4,1664]{2,1,0:T(4,128)(2,1)}), bf16[32,4,1664]{2,1,0:T(4,128)(2,1)S(1)}, u32[]{:S(2)}, u32[]{:S(2)}) async-start(bf16[32,4,1664]{2,1,0:T(4,128)(2,1)} %all_to_all.14), calls=%async_computation.1 | async-start | bytes 851968 | tf_op jit(solution)/shard_map/all_to_all | solution.py:106
  222.0 10.4 %all-to-all-done = bf16[32,4,1664]{2,1,0:T(4,128)(2,1)S(1)} async-done(((bf16[32,4,1664]{2,1,0:T(4,128)(2,1)}), bf16[32,4,1664]{2,1,0:T(4,128)(2,1)S(1)}, u32[]{:S(2)}, u32[]{:S(2)}) %all-to-all-start) | async-done | bytes 426016 | tf_op jit(solution)/shard_map/all_to_all | solution.py:106
  233.7 0.9 all_to_all.16
  234.5 44.4 %all-gather.4.cloned.1.call-done = bf16[1664,3,1664]{2,1,0:T(4,128)(2,1)} async-done(((bf16[52,3,1664]{2,1,0:T(4,128)(2,1)}), bf16[1664,3,1664]{2,1,0:T(4,128)(2,1)}) %all-gather.4.cloned.1.call-update) | async-done | bytes 16613392 | tf_op jit(solution)/shard_map/all_gather | solution.py:111
  278.9 36.4 %copy.43 = bf16[1664,3,1664]{0,2,1:T(8,128)(2,1)} copy(bf16[1664,3,1664]{2,1,0:T(4,128)(2,1)} %all-gather.4.cloned.1.call-done) | data formatting | bytes 33226752 | tf_op jit(solution)/shard_map/all_gather | solution.py:111
  315.3 11.7 %convolution_convert_fusion = bf16[128,4992]{1,0:T(8,128)(2,1)} fusion(bf16[128,1664]{1,0:T(8,128)(2,1)S(1)} %convert_element_type.65, bf16[1664,4992]{0,1:T(8,128)(2,1)} %bitcast.48), kind=kOutput, calls=%fused_computation.15 | convolution fusion | flops 2127151104 | bytes 18317312 | tf_op jit(solution)/shard_map/dot_general | solution.py:112
  327.0 2.6 copy.44
  329.5 2.5 fusion.60
  332.1 2.8 fusion.62
  334.9 2.0 copy.46
  (86 shorter events, 5.6 us)
Async XLA Ops:
  8.0 4.3 %copy-start = (bf16[1024,1664]{1,0:T(8,128)(2,1)S(1)}, bf16[1024,1664]{1,0:T(8,128)(2,1)}, u32[]{:S(2)}) copy-start(bf16[1024,1664]{1,0:T(8,128)(2,1)} %param.24) | copy-start | bytes 10223620
  8.0 4.3 %copy-start.15 = (f32[1024]{0:T(1024)S(1)}, f32[1024]{0:T(1024)}, u32[]{:S(2)}) copy-start(f32[1024]{0:T(1024)} %param.23) | copy-start | bytes 12292
  8.0 4.3 %copy-start.13 = (f32[1664]{0:T(1024)S(1)}, f32[1664]{0:T(1024)}, u32[]{:S(2)}) copy-start(f32[1664]{0:T(1024)} %param.21) | copy-start | bytes 19972
  8.0 155.6 %all-gather.6.cloned.1.call-start = ((), (), s32[]{:S(2)}) async-start(), calls=%async_computation.5 | async-start | bytes 17039360 | tf_op jit(solution)/shard_map/all_gather | solution.py:79
  8.1 3.1 copy-start.3
  8.1 4.2 %copy-start.14 = (f32[1664]{0:T(1024)S(1)}, f32[1664]{0:T(1024)}, u32[]{:S(2)}) copy-start(f32[1664]{0:T(1024)} %param.20) | copy-start | bytes 19972
  12.3 20.6 %copy-start.9 = (s32[1024]{0:T(1024)S(1)}, s32[1024]{0:T(1024)}, u32[]{:S(2)}) copy-start(s32[1024]{0:T(1024)} %param.18) | copy-start | bytes 12292
  12.3 20.6 %copy-start.12 = (s32[2]{0:T(128)S(1)}, s32[2]{0:T(128)}, u32[]{:S(2)}) copy-start(s32[2]{0:T(128)} %constant.155) | copy-start | bytes 28
  12.3 20.7 %copy-start.11 = (s32[2]{0:T(128)S(1)}, s32[2]{0:T(128)}, u32[]{:S(2)}) copy-start(s32[2]{0:T(128)} %constant.158) | copy-start | bytes 28
  32.8 178.1 %reduce-scatter.2.cloned.1.call-start = ((), (), s32[]{:S(2)}) async-start(), calls=%async_computation.3 | async-start | bytes 1064960 | tf_op jit(solution)/shard_map/reduce_scatter | solution.py:84
  163.6 9.7 %copy-start.4 = (bf16[1024,1664]{1,0:T(8,128)(2,1)S(1)}, bf16[1024,1664]{1,0:T(8,128)(2,1)}, u32[]{:S(2)}) copy-start(bf16[1024,1664]{1,0:T(8,128)(2,1)} %param.15) | copy-start | bytes 10223620
  163.6 9.7 %copy-start.8 = (f32[1664]{0:T(1024)S(1)}, f32[1664]{0:T(1024)}, u32[]{:S(2)}) copy-start(f32[1664]{0:T(1024)} %param.25) | copy-start | bytes 19972
  182.6 5.6 %copy-start.5 = (bf16[52,3,1664]{2,0,1:T(8,128)(2,1)S(1)}, bf16[52,3,1664]{2,0,1:T(8,128)(2,1)}, u32[]{:S(2)}) copy-start(bf16[52,3,1664]{2,0,1:T(8,128)(2,1)} %param.29) | copy-start | bytes 1557508
  182.7 6.8 %copy-start.16 = (s32[32]{0:T(128)S(1)}, s32[32]{0:T(128)}, u32[]{:S(2)}) copy-start(s32[32]{0:T(128)} %param.16) | copy-start | bytes 388
  182.7 7.2 %copy-start.2 = (s32[1024]{0:T(1024)S(1)}, s32[1024]{0:T(1024)}, u32[]{:S(2)}) copy-start(s32[1024]{0:T(1024)} %param.19) | copy-start | bytes 12292
  182.7 7.9 %copy-start.10 = (s32[32]{0:T(128)S(1)}, s32[32]{0:T(128)}, u32[]{:S(2)}) copy-start(s32[32]{0:T(128)} %param.17) | copy-start | bytes 388
  188.2 44.9 %copy-start.6 = (f32[1664]{0:T(1024)S(1)}, f32[1664]{0:T(1024)}, u32[]{:S(2)}) copy-start(f32[1664]{0:T(1024)} %param.28) | copy-start | bytes 19972
  188.2 45.0 %copy-start.7 = (f32[1664]{0:T(1024)S(1)}, f32[1664]{0:T(1024)}, u32[]{:S(2)}) copy-start(f32[1664]{0:T(1024)} %param.27) | copy-start | bytes 19972
  188.2 90.7 %all-gather.4.cloned.1.call-start = ((), (), s32[]{:S(2)}) async-start(), calls=%async_computation.4 | async-start | bytes 22843392 | tf_op jit(solution)/shard_map/all_gather | solution.py:111
  213.1 19.4 %all-to-all-start = ((bf16[32,4,1664]{2,1,0:T(4,128)(2,1)}), bf16[32,4,1664]{2,1,0:T(4,128)(2,1)S(1)}, u32[]{:S(2)}, u32[]{:S(2)}) async-start(bf16[32,4,1664]{2,1,0:T(4,128)(2,1)} %all_to_all.14), calls=%async_computation.1 | async-start | bytes 851968 | tf_op jit(solution)/shard_map/all_to_all | solution.py:106
  327.0 9.9 %copy-start.1 = (bf16[1024,1664]{1,0:T(8,128)(2,1)S(1)}, bf16[1024,1664]{1,0:T(8,128)(2,1)}, u32[]{:S(2)}) copy-start(bf16[1024,1664]{1,0:T(8,128)(2,1)} %param.24) | copy-start | bytes 10223620
Sparse Core Ops, SparseCore 0:
  32.9 130.6 all-gather.5
  188.3 22.5 reduce-scatter.1
Sparse Core Ops, SparseCore 1:
  191.3 87.6 all-gather.3
